TPU v7x, 128 devices: a whole 4x4x4 slice. The times are simulated.
128 devices in a mesh: space: 16 (over z, y), pencil: 8 (over x, core).
Axes of the slice: x: 4, y: 4, z: 4, core: 2. Of those that a mesh axis runs over, the one named last changes fastest.
Arguments:
- species: float32 [2048, 53, 1024], P('space', None, 'pencil'), may hold values from 0 to 1
- diffusivity: float32 [53], replicated, may hold values from 0.03 to 0.24
- propagator: float32 [2048, 22472], P('space', 'pencil'), may hold values from -0.03 to 0.92, as said below
- reaction_rate: float32 [2048, 1024], P('space', 'pencil'), may hold values from 0.02 to 0.2
- substeps: int32 [2048, 8], P('space', 'pencil'), may hold values from 1 to 30, as said below
Outputs:
- reacted: float32 [2048, 53, 1024], P('space', None, 'pencil')
Inputs may be any that keep to these rules, and one draw needn't show every extreme that they name: `substeps`: every value lies between 1 and 30, and the largest value, 30, is reached in every draw. `propagator`: each block's matrix has diagonal entries between 0.84 and 0.92 and off-diagonal entries of at most 0.03 in magnitude.
All inputs are finite; a program needn't handle non-finite values.
Results may differ from a plain program's by a relative error of at most 0.0003.
Values sent between devices are 32-bit elements; how exact they have to be, the bound alone decides.
No kernel may reach another device: no remote copies, remote signals or barrier semaphores. Data moves between devices by JAX's collectives and lax.ppermute only.
A program may use at most 128 MiB of HBM per device.

v0:
```python
import jax
import jax.numpy as jnp
from jax import lax
from jax.sharding import PartitionSpec as P


def padded_2(cells, sides, width):
    for axis, dim in sides:
        count = lax.axis_size(axis)
        head = lax.slice_in_dim(cells, 0, width, axis=dim)
        tail = lax.slice_in_dim(cells, cells.shape[dim] - width, cells.shape[dim], axis=dim)
        cells = jnp.concatenate(
            [
                lax.ppermute(tail, axis, [(i, (i + 1) % count) for i in range(count)]),
                cells,
                lax.ppermute(head, axis, [((i + 1) % count, i) for i in range(count)]),
            ],
            axis=dim,
        )
    return cells


def react_blocks(blocks, matrices, rates, count_column):
    row_count = blocks.shape[0]
    nspecies = blocks.shape[1]
    width = blocks.shape[2]
    counts = count_column[:, 0].astype(jnp.int32)
    order = jnp.argsort(-counts, stable=True)
    group_size = 16
    group_count = row_count // group_size
    sorted_blocks = jnp.take(blocks, order, axis=0).reshape(
        group_count, group_size, nspecies, width
    )
    sorted_mats = jnp.take(matrices, order, axis=0).reshape(
        group_count, group_size, nspecies, nspecies
    )
    sorted_rates = jnp.take(rates, order, axis=0).reshape(group_count, group_size, width)
    sorted_counts = jnp.take(counts, order, axis=0).reshape(group_count, group_size)

    def one_group(group_index, finished):
        state = lax.dynamic_index_in_dim(sorted_blocks, group_index, 0, keepdims=False)
        mats = lax.dynamic_index_in_dim(sorted_mats, group_index, 0, keepdims=False)
        rate_rows = lax.dynamic_index_in_dim(sorted_rates, group_index, 0, keepdims=False)
        count_rows = lax.dynamic_index_in_dim(sorted_counts, group_index, 0, keepdims=False)

        def substep(step_index, current):
            pushed = current + rate_rows[:, None, :] * jnp.tanh(current)
            fresh = jnp.einsum("gij,gjc->gic", mats, pushed, precision=lax.Precision.HIGHEST)
            return jnp.where((step_index < count_rows)[:, None, None], fresh, current)

        result_state = lax.fori_loop(0, jnp.max(count_rows), substep, state)
        return lax.dynamic_update_index_in_dim(finished, result_state, group_index, 0)

    finished = lax.fori_loop(0, group_count, one_group, jnp.zeros_like(sorted_blocks))
    inverse = jnp.argsort(order)
    return jnp.take(finished.reshape(row_count, nspecies, width), inverse, axis=0)


def body(species, diffusivity, propagator, reaction_rate, substeps):
    padded = padded_2(species, (("space", 0), ("pencil", 2)), 1)
    neighbours = (
        padded[2:, :, 1:-1] + padded[:-2, :, 1:-1] + padded[1:-1, :, 2:] + padded[1:-1, :, :-2]
    )
    diffused = species + diffusivity[None, :, None] * (neighbours - 4.0 * species)
    count_column = substeps.astype(jnp.float32)
    moved_blocks, moved_mats, moved_rates, moved_counts = (
        lax.all_to_all(diffused, ("space", "pencil"), split_axis=0, concat_axis=0, tiled=True),
        lax.all_to_all(propagator, ("space", "pencil"), split_axis=0, concat_axis=0, tiled=True),
        lax.all_to_all(reaction_rate, ("space", "pencil"), split_axis=0, concat_axis=0, tiled=True),
        lax.all_to_all(count_column, ("space", "pencil"), split_axis=0, concat_axis=0, tiled=True),
    )
    reacted_here = react_blocks(moved_blocks, moved_mats, moved_rates, moved_counts)
    result = lax.all_to_all(
        reacted_here, ("space", "pencil"), split_axis=0, concat_axis=0, tiled=True
    )
    return result


def solution(mesh):
    return jax.shard_map(
        body,
        mesh=mesh,
        in_specs=(
            P("space", None, "pencil"),
            P(),
            P("space", "pencil"),
            P("space", "pencil"),
            P("space", "pencil"),
        ),
        out_specs=P("space", None, "pencil"),
        check_vma=False,
    )
```

profile of v0, /device:TPU:1, one launch (start us, length us, event | category | flops | bytes accessed | tf_op | source)
XLA Modules:
  0.0 392.9 jit_solution(3197344709887548227)
XLA Ops:
  0.0 4.0 %copy.39 = f32[128,53,128]{2,1,0:T(8,128)S(1)} copy(f32[128,53,128]{2,0,1:T(8,128)} %param.11) | data formatting | bytes 6946816 | tf_op args[0]
  9.4 10.7 %all-to-all-start.1 = ((f32[128,1,1]{2,1,0:T(1,128)}), f32[128,1,1]{2,1,0:T(1,128)S(1)}, u32[]{:S(2)}, u32[]{:S(2)}) async-start(f32[128,1,1]{2,1,0:T(1,128)} %copy.28), calls=%async_computation.1 | async-start | bytes 131072 | tf_op jit(solution)/shard_map/all_to_all | solution.py:70
  20.0 5.6 %collective-permute-start = (f32[1,53,128]{2,1,0:T(8,128)}, f32[1,53,128]{2,1,0:T(8,128)}, u32[]{:S(2)}, u32[]{:S(2)}) collective-permute-start(f32[1,53,128]{2,1,0:T(8,128)} %get-tuple-element.181), channel_id=1, source_target_pairs={{8,0},{16,8},{24,16},{32,24},{40,32},{48,40},{56,48},{64,56},{72,6... | collective-permute-start | bytes 81416 | tf_op jit(solution)/shard_map/ppermute | solution.py:16
  30.3 4.7 %all-to-all-start.2 = ((f32[128,1,128]{2,1,0:T(1,128)}), f32[128,1,128]{2,1,0:T(1,128)S(1)}, u32[]{:S(2)}, u32[]{:S(2)}) async-start(f32[128,1,128]{2,1,0:T(1,128)} %bitcast.46), calls=%async_computation.2 | async-start | bytes 131072 | tf_op jit(solution)/shard_map/all_to_all | solution.py:69
  36.4 8.2 %all-to-all-done.2 = f32[128,1,128]{2,1,0:T(1,128)S(1)} async-done(((f32[128,1,128]{2,1,0:T(1,128)}), f32[128,1,128]{2,1,0:T(1,128)S(1)}, u32[]{:S(2)}, u32[]{:S(2)}) %all-to-all-start.2) | async-done | bytes 65568 | tf_op jit(solution)/shard_map/all_to_all | solution.py:69
  44.6 5.2 %all-to-all-start.3 = ((f32[128,1,2809]{2,1,0:T(1,128)}), f32[128,1,2809]{2,1,0:T(1,128)}, u32[]{:S(2)}, u32[]{:S(2)}) async-start(f32[128,1,2809]{2,1,0:T(1,128)} %copy.40), calls=%async_computation.3 | async-start | bytes 2883584 | tf_op jit(solution)/shard_map/all_to_all | solution.py:68
  55.1 7.2 %fusion.13 = (f32[130,53,1]{2,1,0:T(8,128)}, f32[130,53,1]{2,1,0:T(8,128)}) fusion(f32[130,53,128]{2,1,0:T(8,128)} %constant_dynamic-update-slice_fusion), kind=kLoop, calls=%fused_computation.46 | loop fusion | bytes 110240 | tf_op jit(solution)/shard_map/slice | solution.py:10
  62.3 5.0 %copy.34 = f32[130,53,1]{0,2,1:T(1,128)S(1)} copy(f32[130,53,1]{2,1,0:T(8,128)} %get-tuple-element.179) | data formatting | bytes 55120 | tf_op jit(solution)/shard_map/slice | solution.py:10
  68.7 5.0 %copy.36 = f32[130,53,1]{0,2,1:T(1,128)S(1)} copy(f32[130,53,1]{2,1,0:T(8,128)} %get-tuple-element.180) | data formatting | bytes 55120 | tf_op jit(solution)/shard_map/slice | solution.py:11
  74.0 5.8 %copy.35 = f32[130,53,1]{2,1,0:T(8,128)} copy(f32[130,53,1]{0,2,1:T(1,128)S(1)} %collective-permute-done.2) | data formatting | bytes 55120 | tf_op jit(solution)/shard_map/ppermute | solution.py:16
  79.8 5.8 %copy.37 = f32[130,53,1]{2,1,0:T(8,128)} copy(f32[130,53,1]{0,2,1:T(1,128)S(1)} %collective-permute-done.3) | data formatting | bytes 55120 | tf_op jit(solution)/shard_map/ppermute | solution.py:14
  85.6 12.4 %fusion.10 = f32[128,53,128]{2,1,0:T(8,128)} fusion(f32[128,53,128]{2,1,0:T(8,128)} %copy-done, f32[130,53,128]{2,1,0:T(8,128)} %constant_dynamic-update-slice_fusion, f32[130,53,1]{2,1,0:T(8,128)} %copy.37, f32[130,53,1]{2,1,0:T(8,128)} %copy.35, f32[1,53,128]{2,1,0:T(8,128)} %collective-permute-done.1, f32[1,53,128]{2,1,0:T(8,128)} %collective-permute-done, ...), kind=kLoop, calls=%fused_computation.23 | loop fusion | flops 9551872 | bytes 10584100 | tf_op jit(solution)/shard_map/add | solution.py:64
  98.0 11.0 %all-to-all-start = ((f32[128,53,128]{2,1,0:T(8,128)}), f32[128,53,128]{2,1,0:T(8,128)}, u32[]{:S(2)}, u32[]{:S(2)}) async-start(f32[128,53,128]{2,1,0:T(8,128)} %fusion.10), calls=%async_computation | async-start | bytes 7340032 | tf_op jit(solution)/shard_map/all_to_all | solution.py:67
  124.2 4.3 %broadcast_select_fusion.2 = f32[8,16,53,53]{3,2,1,0:T(8,128)} fusion(f32[8,16,53,53]{3,2,1,0:T(8,128)} %gather.26, pred[8,16]{1,0:T(8,128)(4,1)S(1)} %broadcast_in_dim.62), kind=kLoop, calls=%fused_computation.31 | loop fusion | flops 359552 | bytes 2876544 | tf_op jit(solution)/shard_map/jit(_take)/select_n | solution.py:34
  128.5 27.5 %all-to-all-done = f32[128,53,128]{2,1,0:T(8,128)} async-done(((f32[128,53,128]{2,1,0:T(8,128)}), f32[128,53,128]{2,1,0:T(8,128)}, u32[]{:S(2)}, u32[]{:S(2)}) %all-to-all-start) | async-done | bytes 3473440 | tf_op jit(solution)/shard_map/all_to_all | solution.py:67
  156.0 4.7 %gather_fusion.3 = f32[128,53,128]{2,1,0:T(8,128)} fusion(f32[128,53,128]{2,1,0:T(8,128)} %all-to-all-done, s32[1024]{0:T(1024)S(1)} %pad_clamp_fusion.1), kind=kCustom, calls=%fused_computation.clone | custom fusion | bytes 6947328 | tf_op jit(solution)/shard_map/jit(_take)/gather | solution.py:31
  160.7 4.3 %broadcast_select_fusion.1 = f32[128,53,128]{2,1,0:T(8,128)} fusion(f32[128,53,128]{2,1,0:T(8,128)} %gather_fusion.3, pred[128]{0:T(512)(128)(4,1)S(1)} %compare_and_fusion.1), kind=kLoop, calls=%fused_computation.30 | loop fusion | flops 868352 | bytes 6946944 | tf_op jit(solution)/shard_map/jit(_take)/select_n | solution.py:31
  165.0 154.9 %while.36 = (s32[]{:T(128)}, f32[8,16,53,128]{3,2,1,0:T(8,128)}, f32[8,16,53,128]{3,2,1,0:T(8,128)}, s32[8,16]{1,0:T(8,128)S(1)}, f32[8,16,128]{2,1,0:T(8,128)S(...) while((s32[]{:T(128)}, f32[8,16,53,128]{3,2,1,0:T(8,128)}, ...), condition=%wide.region_5.7_spmd, body=%wide.region_1.6_spmd.sunk | while | flops 69359648 | bytes 4062882 | solution.py:54
  167.8 46.3 %while.37 = (s32[]{:T(128)}, f32[16,53,128]{2,1,0:T(8,128)S(1)}, s32[]{:T(128)}, s32[16]{0:T(128)S(1)}, f32[16,128]{1,0:T(8,128)S(1)}, /*index=5*/f32[16,53,53]{2,1,0:T(8,128)S(1)}, s32[]{:T(128)}) while((s32[]{:T(128)}, f32[16,53,128]{2,1,0:T(8,128)S(1)}, s32[]{:T(128)}, s32[16]{0:T(128)S(1)}, f32[16,128]{1,0:T(8,128)S(1)}, ...), condition=%wide.region_4.5_spmd, body=%wide.region_3.4_spmd.sunk | while | flops 69359632 | bytes 1924849 | solution.py:51
  217.7 34.9 %while.37 = (s32[]{:T(128)}, f32[16,53,128]{2,1,0:T(8,128)S(1)}, s32[]{:T(128)}, s32[16]{0:T(128)S(1)}, f32[16,128]{1,0:T(8,128)S(1)}, /*index=5*/f32[16,53,53]{2,1,0:T(8,128)S(1)}, s32[]{:T(128)}) while((s32[]{:T(128)}, f32[16,53,128]{2,1,0:T(8,128)S(1)}, s32[]{:T(128)}, s32[16]{0:T(128)S(1)}, f32[16,128]{1,0:T(8,128)S(1)}, ...), condition=%wide.region_4.5_spmd, body=%wide.region_3.4_spmd.sunk | while | flops 69359632 | bytes 1924849 | solution.py:51
  256.2 23.5 %while.37 = (s32[]{:T(128)}, f32[16,53,128]{2,1,0:T(8,128)S(1)}, s32[]{:T(128)}, s32[16]{0:T(128)S(1)}, f32[16,128]{1,0:T(8,128)S(1)}, /*index=5*/f32[16,53,53]{2,1,0:T(8,128)S(1)}, s32[]{:T(128)}) while((s32[]{:T(128)}, f32[16,53,128]{2,1,0:T(8,128)S(1)}, s32[]{:T(128)}, s32[16]{0:T(128)S(1)}, f32[16,128]{1,0:T(8,128)S(1)}, ...), condition=%wide.region_4.5_spmd, body=%wide.region_3.4_spmd.sunk | while | flops 69359632 | bytes 1924849 | solution.py:51
  283.3 12.0 %while.37 = (s32[]{:T(128)}, f32[16,53,128]{2,1,0:T(8,128)S(1)}, s32[]{:T(128)}, s32[16]{0:T(128)S(1)}, f32[16,128]{1,0:T(8,128)S(1)}, /*index=5*/f32[16,53,53]{2,1,0:T(8,128)S(1)}, s32[]{:T(128)}) while((s32[]{:T(128)}, f32[16,53,128]{2,1,0:T(8,128)S(1)}, s32[]{:T(128)}, s32[16]{0:T(128)S(1)}, f32[16,128]{1,0:T(8,128)S(1)}, ...), condition=%wide.region_4.5_spmd, body=%wide.region_3.4_spmd.sunk | while | flops 69359632 | bytes 1924849 | solution.py:51
  319.8 4.7 %gather_fusion.4 = f32[128,53,128]{2,1,0:T(8,128)} fusion(f32[128,53,128]{2,1,0:T(8,128)} %bitcast.43, s32[1024]{0:T(1024)S(1)} %pad_clamp_fusion), kind=kCustom, calls=%fused_computation.1.clone | custom fusion | bytes 6947328 | tf_op jit(solution)/shard_map/jit(_take)/gather | solution.py:56
  326.9 63.6 %all_to_all.43 = f32[128,53,128]{2,1,0:T(8,128)S(1)} all-to-all(f32[128,53,128]{2,1,0:T(8,128)S(1)} %broadcast_select_fusion), channel_id=1, replica_groups=mesh['space'=16,'pencil'=8] {'space','pencil'}, dimensions={0} | all-to-all | bytes 6946816 | tf_op jit(solution)/shard_map/all_to_all | solution.py:73
  (318 shorter events, 147.2 us)
Async XLA Ops:
  0.0 8.6 %copy-start.5 = (s32[128,1]{0,1:T(1,128)S(1)}, s32[128,1]{0,1:T(1,128)}, u32[]{:S(2)}) copy-start(s32[128,1]{0,1:T(1,128)} %param.15) | copy-start | bytes 1540
  4.0 1.9 copy-start
  5.9 43.9 %copy-start.1 = (f32[128,53,128]{2,0,1:T(8,128)S(1)}, f32[128,53,128]{2,0,1:T(8,128)}, u32[]{:S(2)}) copy-start(f32[128,53,128]{2,0,1:T(8,128)} %param.11) | copy-start | bytes 10420228
  6.5 28.5 %collective-permute-start.1 = (f32[1,53,128]{2,1,0:T(8,128)}, f32[1,53,128]{2,1,0:T(8,128)}, u32[]{:S(2)}, u32[]{:S(2)}) collective-permute-start(f32[1,53,128]{2,1,0:T(8,128)} %get-tuple-element.182), channel_id=1, source_target_pairs={{0,8},{8,16},{16,24},{24,32},{32,40},{40,48},{48,56},{56,64},{64,7... | collective-permute-start | bytes 81416 | tf_op jit(solution)/shard_map/ppermute | solution.py:14
  9.4 20.3 %all-to-all-start.1 = ((f32[128,1,1]{2,1,0:T(1,128)}), f32[128,1,1]{2,1,0:T(1,128)S(1)}, u32[]{:S(2)}, u32[]{:S(2)}) async-start(f32[128,1,1]{2,1,0:T(1,128)} %copy.28), calls=%async_computation.1 | async-start | bytes 131072 | tf_op jit(solution)/shard_map/all_to_all | solution.py:70
  20.0 33.7 %collective-permute-start = (f32[1,53,128]{2,1,0:T(8,128)}, f32[1,53,128]{2,1,0:T(8,128)}, u32[]{:S(2)}, u32[]{:S(2)}) collective-permute-start(f32[1,53,128]{2,1,0:T(8,128)} %get-tuple-element.181), channel_id=1, source_target_pairs={{8,0},{16,8},{24,16},{32,24},{40,32},{48,40},{56,48},{64,56},{72,6... | collective-permute-start | bytes 81416 | tf_op jit(solution)/shard_map/ppermute | solution.py:16
  29.7 0.6 copy-start.2
  30.3 14.3 %all-to-all-start.2 = ((f32[128,1,128]{2,1,0:T(1,128)}), f32[128,1,128]{2,1,0:T(1,128)S(1)}, u32[]{:S(2)}, u32[]{:S(2)}) async-start(f32[128,1,128]{2,1,0:T(1,128)} %bitcast.46), calls=%async_computation.2 | async-start | bytes 131072 | tf_op jit(solution)/shard_map/all_to_all | solution.py:69
  44.6 53.4 %all-to-all-start.3 = ((f32[128,1,2809]{2,1,0:T(1,128)}), f32[128,1,2809]{2,1,0:T(1,128)}, u32[]{:S(2)}, u32[]{:S(2)}) async-start(f32[128,1,2809]{2,1,0:T(1,128)} %copy.40), calls=%async_computation.3 | async-start | bytes 2883584 | tf_op jit(solution)/shard_map/all_to_all | solution.py:68
  67.2 6.8 %collective-permute-start.2 = (f32[130,53,1]{0,2,1:T(1,128)S(1)}, f32[130,53,1]{0,2,1:T(1,128)S(1)}, u32[]{:S(2)}, u32[]{:S(2)}) collective-permute-start(f32[130,53,1]{0,2,1:T(1,128)S(1)} %copy.34), channel_id=1, source_target_pairs={{1,0},{2,1},{3,2},{4,3},{5,4},{6,5},{7,6},{0,7},{9,8},{10,9},{11,1... | collective-permute-start | bytes 82688 | tf_op jit(solution)/shard_map/ppermute | solution.py:16
  73.7 11.9 %copy-start.4 = (f32[53]{0:T(128)S(1)}, f32[53]{0:T(128)}, u32[]{:S(2)}) copy-start(f32[53]{0:T(128)} %param.12) | copy-start | bytes 640
  73.7 6.1 %collective-permute-start.3 = (f32[130,53,1]{0,2,1:T(1,128)S(1)}, f32[130,53,1]{0,2,1:T(1,128)S(1)}, u32[]{:S(2)}, u32[]{:S(2)}) collective-permute-start(f32[130,53,1]{0,2,1:T(1,128)S(1)} %copy.36), channel_id=1, source_target_pairs={{0,1},{1,2},{2,3},{3,4},{4,5},{5,6},{6,7},{7,0},{8,9},{9,10},{10,1... | collective-permute-start | bytes 82688 | tf_op jit(solution)/shard_map/ppermute | solution.py:14
  98.0 11.0 %copy-start.3 = (f32[128,1,1]{2,1,0:T(1,128)S(1)}, f32[128,1,1]{2,1,0:T(1,128)}, u32[]{:S(2)}) copy-start(f32[128,1,1]{2,1,0:T(1,128)} %copy-done.2) | copy-start | bytes 1540
  98.0 58.0 %all-to-all-start = ((f32[128,53,128]{2,1,0:T(8,128)}), f32[128,53,128]{2,1,0:T(8,128)}, u32[]{:S(2)}, u32[]{:S(2)}) async-start(f32[128,53,128]{2,1,0:T(8,128)} %fusion.10), calls=%async_computation | async-start | bytes 7340032 | tf_op jit(solution)/shard_map/all_to_all | solution.py:67
where the time goes:
time: 395 us; the launch traced here: 393 us
  local copies, waits for them, and re-layouts  92.2 us (23%)
  matrix products  68 us (17%)
  blocking collectives  63.6 us (16%)
  loops' own time  55.1 us (14%)
  starting transfers between devices  41 us (10%)
  other arithmetic  37 us (9%)
  waiting for transfers between devices  35.8 us (9%)
    dot_general x74, matrix products, substep(): jnp.einsum('gij,gjc->gic', mats, pushed, precision=lax.Precision.HIGHEST)  68 us
    all_to_all x1, blocking collectives, body(): lax.all_to_all(reacted_here, ('space', 'pencil'), split_axis=0, concat_ax...  63.6 us
    another operation x8, loops' own time, one_group(): result_state = lax.fori_loop(0, jnp.max(count_rows), substep, state)  54.9 us
    all_to_all x1, waiting for transfers between devices, body(): lax.all_to_all(diffused, ('space', 'pencil'), split_axis=0, concat_axis=0...  27.5 us
    unnamed x16, local copies, waits for them, and re-layouts  13.3 us
    slice x3, local copies, waits for them, and re-layouts, padded_2(): head = lax.slice_in_dim(cells, 0, width, axis=dim)  12.7 us
    add x1, other arithmetic, body(): species + diffusivity[None, :, None] * (neighbours - 4.0 * species)  12.4 us
    all_to_all x1, starting transfers between devices, body(): lax.all_to_all(diffused, ('space', 'pencil'), split_axis=0, concat_axis=0...  11 us
  transfers between devices with their start and end apart: 8, of which 3 were waited for; matrix products, arithmetic and copies ran while one was open for 18% of the time, Pallas kernels for 0%

commit v1 on v0

v1 whole, which is shorter than its diff:
```python
import functools

import jax
import jax.numpy as jnp
from jax import lax
from jax.experimental import pallas as pl
from jax.experimental.pallas import tpu as pltpu
from jax.sharding import PartitionSpec as P

EDGE_ROWS = 16
PREP_ROWS = 16
GROUP = 32
UNROLL = 4
LANES = 128


def edges_kernel(nspec, cells, first_col, last_col, first_row, last_row):
    step = pl.program_id(0)
    lane = lax.broadcasted_iota(jnp.int32, (EDGE_ROWS, LANES), 1)
    first = jnp.zeros((EDGE_ROWS, LANES), jnp.float32)
    last = jnp.zeros((EDGE_ROWS, LANES), jnp.float32)
    for s in range(nspec):
        here = cells[s]
        first = jnp.where(lane == s, pltpu.roll(here, s, 1), first)
        last = jnp.where(lane == s, pltpu.roll(here, s + 1, 1), last)
    first_col[...] = first
    last_col[...] = last

    @pl.when(step == 0)
    def _():
        first_row[...] = cells[:, 0, :]

    @pl.when(step == pl.num_programs(0) - 1)
    def _():
        last_row[...] = cells[:, EDGE_ROWS - 1, :]


def matrices_kernel(nspec, pad, prop, lhs, rows):
    width = nspec * nspec
    lane = lax.broadcasted_iota(jnp.int32, (PREP_ROWS, LANES), 1)

    def window(start):
        if start + LANES <= width:
            return prop[:, start : start + LANES]
        tail = prop[:, start:width]
        return jnp.concatenate([tail, jnp.zeros((PREP_ROWS, start + LANES - width), jnp.float32)], axis=1)

    for i in range(nspec, pad):
        rows[pl.ds(i, PREP_ROWS, stride=pad), :] = jnp.zeros((PREP_ROWS, LANES), jnp.float32)
    for i in range(nspec):
        start = i * nspec // LANES * LANES
        skip = i * nspec - start
        piece = window(start)
        if skip:
            piece = pltpu.roll(piece, LANES - skip, 1)
        if skip + nspec > LANES:
            piece = jnp.where(lane < LANES - skip, piece, pltpu.roll(window(start + LANES), LANES - skip, 1))
        rows[pl.ds(i, PREP_ROWS, stride=pad), :] = jnp.where(lane < nspec, piece, 0.0)
    for g in range(PREP_ROWS):
        mat = rows[g * pad : (g + 1) * pad, :]
        high = mat.astype(jnp.bfloat16).astype(jnp.float32)
        both = jnp.concatenate([high, mat - high], axis=0)
        both = both + pltpu.roll(both, LANES // 2, 1)
        k = g % 2
        lhs[g // 2, :, k * LANES : (k + 1) * LANES] = both.astype(jnp.bfloat16)


def react_kernel(nspec, pad, counts, coef, cells, top, bottom, left, right, lhs, rate, out, state):
    rows_total = cells.shape[1]
    base = pl.program_id(0) * GROUP
    lane = lax.broadcasted_iota(jnp.int32, (GROUP, LANES), 1)
    sub = lax.broadcasted_iota(jnp.int32, (GROUP, LANES), 0)
    at_top = base == 0
    at_bottom = base + GROUP == rows_total
    row_above = jnp.maximum(base - 1, 0)
    row_below = jnp.minimum(base + GROUP, rows_total - 1)
    left_cols = left[pl.ds(base, GROUP), :]
    right_cols = right[pl.ds(base, GROUP), :]

    for s in range(nspec, pad):
        state[pl.ds(s, GROUP, stride=pad), :] = jnp.zeros((GROUP, LANES), jnp.float32)
    for s in range(nspec):
        here = cells[s, pl.ds(base, GROUP), :]
        before = jnp.where(at_top, top[s : s + 1, :], cells[s, pl.ds(row_above, 1), :])
        after = jnp.where(at_bottom, bottom[s : s + 1, :], cells[s, pl.ds(row_below, 1), :])
        above = jnp.where(sub == 0, before, pltpu.roll(here, 1, 0))
        below = jnp.where(sub == GROUP - 1, after, pltpu.roll(here, GROUP - 1, 0))
        edge_l = pltpu.roll(left_cols, LANES - 1 - s, 1)
        edge_r = pltpu.roll(right_cols, (LANES - s) % LANES, 1) if s else right_cols
        from_l = pltpu.roll(jnp.where(lane == LANES - 1, edge_l, here), 1, 1)
        from_r = pltpu.roll(jnp.where(lane == 0, edge_r, here), LANES - 1, 1)
        moved = here + coef[s] * ((above + below) + (from_l + from_r) - 4.0 * here)
        state[pl.ds(s, GROUP, stride=pad), :] = moved

    most = counts[base]
    for g in range(1, GROUP):
        most = jnp.maximum(most, counts[base + g])

    tail_rows = jnp.zeros((LANES // 2 - pad, LANES), jnp.float32)
    nothing = jnp.zeros((LANES, LANES), jnp.bfloat16)

    def parts(g):
        now = state[g * pad : (g + 1) * pad, :]
        pushed = now + rate[g : g + 1, :] * jnp.tanh(now)
        full = jnp.concatenate([pushed, tail_rows], axis=0)
        high = full.astype(jnp.bfloat16)
        low = (full - high.astype(jnp.float32)).astype(jnp.bfloat16)
        return jnp.concatenate([high, low], axis=0)

    def substep(step):
        for p in range(GROUP // 2):
            rhs = jnp.concatenate(
                [
                    jnp.concatenate([parts(2 * p), nothing], axis=1),
                    jnp.concatenate([nothing, parts(2 * p + 1)], axis=1),
                ],
                axis=0,
            )
            sums = jnp.dot(lhs[p], rhs, preferred_element_type=jnp.float32)
            sums = sums[0:pad] + sums[pad : 2 * pad]
            for k in range(2):
                g = 2 * p + k
                mask = jnp.broadcast_to(step < counts[base + g], (pad, LANES))
                pltpu.store(state.at[pl.ds(g * pad, pad), :], sums[:, k * LANES : (k + 1) * LANES], mask=mask)

    def several(i, carry):
        for u in range(UNROLL):
            substep(i * UNROLL + u)
        return carry

    def single(i, carry):
        substep(i)
        return carry

    whole = most // UNROLL
    lax.fori_loop(0, whole, several, 0)
    lax.fori_loop(whole * UNROLL, most, single, 0)

    for s in range(nspec):
        out[s] = state[pl.ds(s, GROUP, stride=pad), :]


def body(species, diffusivity, propagator, reaction_rate, substeps):
    rows, nspec, lanes = species.shape
    pad = (nspec + 7) // 8 * 8
    f32 = jnp.float32
    cells = species.transpose(1, 0, 2)

    def shift(values, axis, up):
        count = lax.axis_size(axis)
        pairs = [(i, (i + 1) % count) if up else ((i + 1) % count, i) for i in range(count)]
        return lax.ppermute(values, axis, pairs)

    first_col, last_col, first_row, last_row = pl.pallas_call(
        functools.partial(edges_kernel, nspec),
        name="edges",
        grid=(rows // EDGE_ROWS,),
        in_specs=[pl.BlockSpec((nspec, EDGE_ROWS, lanes), lambda i: (0, i, 0))],
        out_specs=[
            pl.BlockSpec((EDGE_ROWS, lanes), lambda i: (i, 0)),
            pl.BlockSpec((EDGE_ROWS, lanes), lambda i: (i, 0)),
            pl.BlockSpec((nspec, lanes), lambda i: (0, 0)),
            pl.BlockSpec((nspec, lanes), lambda i: (0, 0)),
        ],
        out_shape=[jax.ShapeDtypeStruct((rows, lanes), f32)] * 2 + [jax.ShapeDtypeStruct((nspec, lanes), f32)] * 2,
        compiler_params=pltpu.CompilerParams(vmem_limit_bytes=8 << 20),
        cost_estimate=pl.CostEstimate(flops=1 << 20, bytes_accessed=4 << 20, transcendentals=0),
    )(cells)

    top = shift(last_row, "space", True)
    bottom = shift(first_row, "space", False)
    left = shift(last_col, "pencil", True)
    right = shift(first_col, "pencil", False)

    lhs = pl.pallas_call(
        functools.partial(matrices_kernel, nspec, pad),
        name="matrices",
        grid=(rows // PREP_ROWS,),
        in_specs=[pl.BlockSpec((PREP_ROWS, nspec * nspec), lambda i: (i, 0))],
        out_specs=pl.BlockSpec((PREP_ROWS // 2, 2 * pad, 2 * lanes), lambda i: (i, 0, 0)),
        out_shape=jax.ShapeDtypeStruct((rows // 2, 2 * pad, 2 * lanes), jnp.bfloat16),
        scratch_shapes=[pltpu.VMEM((PREP_ROWS * pad, lanes), f32)],
        compiler_params=pltpu.CompilerParams(vmem_limit_bytes=8 << 20),
        cost_estimate=pl.CostEstimate(flops=1 << 24, bytes_accessed=6 << 20, transcendentals=0),
    )(propagator)

    once = pl.Buffered(1)
    result = pl.pallas_call(
        functools.partial(react_kernel, nspec, pad),
        name="react",
        out_shape=jax.ShapeDtypeStruct((nspec, rows, lanes), f32),
        grid_spec=pltpu.PrefetchScalarGridSpec(
            num_scalar_prefetch=2,
            grid=(rows // GROUP,),
            in_specs=[
                pl.BlockSpec((nspec, rows, lanes), lambda i, c, d: (0, 0, 0), pipeline_mode=once),
                pl.BlockSpec((nspec, lanes), lambda i, c, d: (0, 0), pipeline_mode=once),
                pl.BlockSpec((nspec, lanes), lambda i, c, d: (0, 0), pipeline_mode=once),
                pl.BlockSpec((rows, lanes), lambda i, c, d: (0, 0), pipeline_mode=once),
                pl.BlockSpec((rows, lanes), lambda i, c, d: (0, 0), pipeline_mode=once),
                pl.BlockSpec((GROUP // 2, 2 * pad, 2 * lanes), lambda i, c, d: (i, 0, 0)),
                pl.BlockSpec((GROUP, lanes), lambda i, c, d: (i, 0)),
            ],
            out_specs=pl.BlockSpec((nspec, GROUP, lanes), lambda i, c, d: (0, i, 0)),
            scratch_shapes=[pltpu.VMEM((GROUP * pad, lanes), f32)],
        ),
        compiler_params=pltpu.CompilerParams(vmem_limit_bytes=24 << 20),
        cost_estimate=pl.CostEstimate(flops=20 * rows * 2 * pad * 256 * 256, bytes_accessed=9 << 20, transcendentals=0),
    )(substeps.reshape(rows), diffusivity, cells, top, bottom, left, right, lhs, reaction_rate)
    return result.transpose(1, 0, 2)


def solution(mesh):
    return jax.shard_map(
        body,
        mesh=mesh,
        in_specs=(
            P("space", None, "pencil"),
            P(),
            P("space", "pencil"),
            P("space", "pencil"),
            P("space", "pencil"),
        ),
        out_specs=P("space", None, "pencil"),
        check_vma=False,
    )
```

time: 395 us -> 74.2 us (0.19)
  the two profiles are of different devices: /device:TPU:1 before, /device:TPU:96 now
where the time goes in v1:
time: 74.2 us; the launch traced here: 75.3 us
  Pallas kernels  64.7 us (87%)
  starting transfers between devices  7.09 us (10%)
  local copies, waits for them, and re-layouts  3.36 us (5%)
    pallas_call x1, Pallas kernels, body(): pl.pallas_call(functools.partial(react_kernel, nspec, pad), name='react',...  58.2 us
    ppermute x4, starting transfers between devices, shift(): return lax.ppermute(values, axis, pairs)  7.09 us
    pallas_call x1, Pallas kernels, body(): pl.pallas_call(functools.partial(matrices_kernel, nspec, pad), name='matr...  3.89 us
    unnamed x12, local copies, waits for them, and re-layouts  3.36 us
    pallas_call x1, Pallas kernels, body(): pl.pallas_call(functools.partial(edges_kernel, nspec), name='edges', grid...  2.66 us
  transfers between devices with their start and end apart: 4, of which 0 were waited for; matrix products, arithmetic and copies ran while one was open for 0% of the time, Pallas kernels for 5%

profile of v1, /device:TPU:96, one launch (start us, length us, event | category | flops | bytes accessed | tf_op | source)
XLA Modules:
  0.0 75.3 jit_solution(15558241286639827231)
XLA Ops:
  0.0 0.0 copy-start
  0.0 2.0 %copy-done = f32[128,53,128]{2,0,1:T(8,128)S(1)} copy-done((f32[128,53,128]{2,0,1:T(8,128)S(1)}, f32[128,53,128]{2,0,1:T(8,128)}, u32[]{:S(2)}) %copy-start) | copy-done | bytes 3473432
  2.0 0.0 copy-start.1
  2.0 0.0 copy-start.4
  2.0 0.0 copy-start.5
  2.0 2.7 %edges.1 = (f32[128,128]{1,0:T(8,128)S(1)}, f32[128,128]{1,0:T(8,128)S(1)}, f32[53,128]{1,0:T(8,128)S(1)}, f32[53,128]{1,0:T(8,128)S(1)}) custom-call(f32[53,128,128]{2,1,0:T(8,128)S(1)} %bitcast.3), custom_call_target="tpu_custom_call" | custom-call | flops 1048576 | bytes 4194304 | tf_op jit(solution)/shard_map/edges/pallas_call | solution.py:154
  4.7 0.0 collective-permute-start.2
  4.7 2.9 %collective-permute-start.3 = (f32[128,128]{1,0:T(8,128)S(1)}, f32[128,128]{1,0:T(8,128)S(1)}, u32[]{:S(2)}, u32[]{:S(2)}) collective-permute-start(f32[128,128]{1,0:T(8,128)S(1)} %get-tuple-element.12), channel_id=1, source_target_pairs={{1,0},{2,1},{3,2},{4,3},{5,4},{6,5},{7,6},{0,7},{9,8},{10,9},{11,1... | collective-permute-start | bytes 196616 | tf_op jit(solution)/shard_map/ppermute | solution.py:152
  7.6 1.6 %collective-permute-start = (f32[53,128]{1,0:T(8,128)S(1)}, f32[53,128]{1,0:T(8,128)S(1)}, u32[]{:S(2)}, u32[]{:S(2)}) collective-permute-start(f32[53,128]{1,0:T(8,128)S(1)} %get-tuple-element.9), channel_id=1, source_target_pairs={{0,8},{8,16},{16,24},{24,32},{32,40},{40,48},{48,56},{56,64},{64,7... | collective-permute-start | bytes 81416 | tf_op jit(solution)/shard_map/ppermute | solution.py:152
  9.2 2.6 %collective-permute-start.1 = (f32[53,128]{1,0:T(8,128)S(1)}, f32[53,128]{1,0:T(8,128)S(1)}, u32[]{:S(2)}, u32[]{:S(2)}) collective-permute-start(f32[53,128]{1,0:T(8,128)S(1)} %get-tuple-element.10), channel_id=1, source_target_pairs={{8,0},{16,8},{24,16},{32,24},{40,32},{48,40},{56,48},{64,56},{72,6... | collective-permute-start | bytes 81416 | tf_op jit(solution)/shard_map/ppermute | solution.py:152
  11.8 0.0 copy-start.2
  11.8 1.4 %copy-done.2 = f32[128,2809]{1,0:T(8,128)S(1)} copy-done((f32[128,2809]{1,0:T(8,128)S(1)}, f32[128,2809]{1,0:T(8,128)}, u32[]{:S(2)}) %copy-start.2) | copy-done | bytes 1438232
  13.1 0.0 copy-start.3
  13.1 3.9 %matrices.1.lhs = bf16[64,112,256]{2,1,0:T(8,128)(2,1)S(1)} custom-call(f32[128,2809]{1,0:T(8,128)S(1)} %copy-done.2), custom_call_target="tpu_custom_call" | custom-call | flops 16777216 | bytes 6291456 | tf_op jit(solution)/shard_map/matrices/pallas_call | solution.py:175
  17.0 0.0 collective-permute-done.top
  17.0 0.0 collective-permute-done.1.bottom
  17.0 0.0 collective-permute-done.2.left
  17.1 0.0 collective-permute-done.3.right
  17.1 0.0 copy-done.1
  17.1 0.0 copy-done.4
  17.1 0.0 copy-done.5
  17.1 0.0 copy-done.3
  17.1 58.2 %react.1 = f32[53,128,128]{2,1,0:T(8,128)} custom-call(s32[128]{0:T(128)S(1)} %bitcast.5, f32[53]{0:T(128)S(1)} %copy-done.5, f32[53,128,128]{2,1,0:T(8,128)S(1)} %bitcast.4, f32[53,128]{1,0:T(8,128)S(1)} %collective-permute-done.top, f32[53,128]{1,0:T(8,128)S(1)} %collective-permute-done.1.bottom, f32[128,128]{1,0:T(8,128)S(1)} %collective-permute-done.2.left, ...), custom_call_target="tpu_custom_call" | custom-call | flops 18790481920 | bytes 9437184 | tf_op jit(solution)/shard_map/react/pallas_call | solution.py:188
Async XLA Ops:
  0.0 2.0 %copy-start = (f32[128,53,128]{2,0,1:T(8,128)S(1)}, f32[128,53,128]{2,0,1:T(8,128)}, u32[]{:S(2)}) copy-start(f32[128,53,128]{2,0,1:T(8,128)} %param.5) | copy-start | bytes 10420228
  2.0 15.1 %copy-start.1 = (f32[128,53,128]{2,0,1:T(8,128)S(1)}, f32[128,53,128]{2,0,1:T(8,128)}, u32[]{:S(2)}) copy-start(f32[128,53,128]{2,0,1:T(8,128)} %param.5) | copy-start | bytes 10420228
  2.0 15.1 %copy-start.4 = (s32[128,1]{0,1:T(1,128)S(1)}, s32[128,1]{0,1:T(1,128)}, u32[]{:S(2)}) copy-start(s32[128,1]{0,1:T(1,128)} %param.9) | copy-start | bytes 1540
  2.0 15.1 %copy-start.5 = (f32[53]{0:T(128)S(1)}, f32[53]{0:T(128)}, u32[]{:S(2)}) copy-start(f32[53]{0:T(128)} %coef.1) | copy-start | bytes 640
  4.7 12.4 %collective-permute-start.2 = (f32[128,128]{1,0:T(8,128)S(1)}, f32[128,128]{1,0:T(8,128)S(1)}, u32[]{:S(2)}, u32[]{:S(2)}) collective-permute-start(f32[128,128]{1,0:T(8,128)S(1)} %get-tuple-element.11), channel_id=1, source_target_pairs={{0,1},{1,2},{2,3},{3,4},{4,5},{5,6},{6,7},{7,0},{8,9},{9,10},{10,1... | collective-permute-start | bytes 196616 | tf_op jit(solution)/shard_map/ppermute | solution.py:152
  4.7 12.4 %collective-permute-start.3 = (f32[128,128]{1,0:T(8,128)S(1)}, f32[128,128]{1,0:T(8,128)S(1)}, u32[]{:S(2)}, u32[]{:S(2)}) collective-permute-start(f32[128,128]{1,0:T(8,128)S(1)} %get-tuple-element.12), channel_id=1, source_target_pairs={{1,0},{2,1},{3,2},{4,3},{5,4},{6,5},{7,6},{0,7},{9,8},{10,9},{11,1... | collective-permute-start | bytes 196616 | tf_op jit(solution)/shard_map/ppermute | solution.py:152
  7.6 9.4 %collective-permute-start = (f32[53,128]{1,0:T(8,128)S(1)}, f32[53,128]{1,0:T(8,128)S(1)}, u32[]{:S(2)}, u32[]{:S(2)}) collective-permute-start(f32[53,128]{1,0:T(8,128)S(1)} %get-tuple-element.9), channel_id=1, source_target_pairs={{0,8},{8,16},{16,24},{24,32},{32,40},{40,48},{48,56},{56,64},{64,7... | collective-permute-start | bytes 81416 | tf_op jit(solution)/shard_map/ppermute | solution.py:152
  9.2 7.8 %collective-permute-start.1 = (f32[53,128]{1,0:T(8,128)S(1)}, f32[53,128]{1,0:T(8,128)S(1)}, u32[]{:S(2)}, u32[]{:S(2)}) collective-permute-start(f32[53,128]{1,0:T(8,128)S(1)} %get-tuple-element.10), channel_id=1, source_target_pairs={{8,0},{16,8},{24,16},{32,24},{40,32},{48,40},{56,48},{64,56},{72,6... | collective-permute-start | bytes 81416 | tf_op jit(solution)/shard_map/ppermute | solution.py:152
  11.8 1.4 %copy-start.2 = (f32[128,2809]{1,0:T(8,128)S(1)}, f32[128,2809]{1,0:T(8,128)}, u32[]{:S(2)}) copy-start(f32[128,2809]{1,0:T(8,128)} %prop.1) | copy-start | bytes 4314628
  13.1 4.0 %copy-start.3 = (f32[128,128]{1,0:T(8,128)S(1)}, f32[128,128]{1,0:T(8,128)}, u32[]{:S(2)}) copy-start(f32[128,128]{1,0:T(8,128)} %rate.1) | copy-start | bytes 196612

commit v2 on v1

--- a/solution.py
+++ b/solution.py
@@ -7,36 +7,38 @@
 from jax.experimental.pallas import tpu as pltpu
 from jax.sharding import PartitionSpec as P
 
-EDGE_ROWS = 16
+CHUNKS = 6
 PREP_ROWS = 16
 GROUP = 32
-UNROLL = 4
+UNROLLS = (8, 4, 2, 1)
 LANES = 128
 
 
-def edges_kernel(nspec, cells, first_col, last_col, first_row, last_row):
-    step = pl.program_id(0)
-    lane = lax.broadcasted_iota(jnp.int32, (EDGE_ROWS, LANES), 1)
-    first = jnp.zeros((EDGE_ROWS, LANES), jnp.float32)
-    last = jnp.zeros((EDGE_ROWS, LANES), jnp.float32)
-    for s in range(nspec):
-        here = cells[s]
-        first = jnp.where(lane == s, pltpu.roll(here, s, 1), first)
-        last = jnp.where(lane == s, pltpu.roll(here, s + 1, 1), last)
-    first_col[...] = first
-    last_col[...] = last
-
-    @pl.when(step == 0)
-    def _():
-        first_row[...] = cells[:, 0, :]
-
-    @pl.when(step == pl.num_programs(0) - 1)
-    def _():
-        last_row[...] = cells[:, EDGE_ROWS - 1, :]
+def edges_kernel(nspec, source, cells, cols, first_row, last_row, sems):
+    rows = cells.shape[1]
+    cuts = [nspec * k // CHUNKS for k in range(CHUNKS + 1)]
+    copies = []
+    for k in range(CHUNKS):
+        part = pl.ds(cuts[k], cuts[k + 1] - cuts[k])
+        copies.append(pltpu.make_async_copy(source.at[part], cells.at[part], sems.at[k]))
+        copies[-1].start()
+    lane = lax.broadcasted_iota(jnp.int32, (8, LANES), 1)
+    for k in range(CHUNKS):
+        copies[k].wait()
+        picks = [(lane == 2 * s) | (lane == (2 * s - 1) % LANES) for s in range(cuts[k], cuts[k + 1])]
+        for r in range(0, rows, 8):
+            held = jnp.zeros((8, LANES), jnp.float32) if k == 0 else cols[r : r + 8, :]
+            for pick, s in zip(picks, range(cuts[k], cuts[k + 1])):
+                here = cells[s, r : r + 8, :]
+                held = jnp.where(pick, pltpu.roll(here, 2 * s, 1) if s else here, held)
+            cols[r : r + 8, :] = held
+    first_row[...] = cells[:, 0, :]
+    last_row[...] = cells[:, rows - 1, :]
 
 
 def matrices_kernel(nspec, pad, prop, lhs, rows):
     width = nspec * nspec
+    half = LANES // 2
     lane = lax.broadcasted_iota(jnp.int32, (PREP_ROWS, LANES), 1)
 
     def window(start):
@@ -51,16 +53,16 @@
         start = i * nspec // LANES * LANES
         skip = i * nspec - start
         piece = window(start)
-        if skip:
-            piece = pltpu.roll(piece, LANES - skip, 1)
         if skip + nspec > LANES:
-            piece = jnp.where(lane < LANES - skip, piece, pltpu.roll(window(start + LANES), LANES - skip, 1))
-        rows[pl.ds(i, PREP_ROWS, stride=pad), :] = jnp.where(lane < nspec, piece, 0.0)
+            piece = jnp.where(lane >= skip, piece, window(start + LANES))
+        once = pltpu.roll(piece, LANES - skip, 1) if skip else piece
+        again = pltpu.roll(piece, (half - skip) % LANES, 1) if skip != half else piece
+        twice = jnp.where(lane < nspec, once, jnp.where((lane >= half) & (lane < half + nspec), again, 0.0))
+        rows[pl.ds(i, PREP_ROWS, stride=pad), :] = twice
     for g in range(PREP_ROWS):
         mat = rows[g * pad : (g + 1) * pad, :]
         high = mat.astype(jnp.bfloat16).astype(jnp.float32)
         both = jnp.concatenate([high, mat - high], axis=0)
-        both = both + pltpu.roll(both, LANES // 2, 1)
         k = g % 2
         lhs[g // 2, :, k * LANES : (k + 1) * LANES] = both.astype(jnp.bfloat16)
 
@@ -74,8 +76,11 @@
     at_bottom = base + GROUP == rows_total
     row_above = jnp.maximum(base - 1, 0)
     row_below = jnp.minimum(base + GROUP, rows_total - 1)
-    left_cols = left[pl.ds(base, GROUP), :]
-    right_cols = right[pl.ds(base, GROUP), :]
+    edge_cols = jnp.where(
+        lane % 2 == 0,
+        pltpu.roll(left[pl.ds(base, GROUP), :], 1, 1),
+        pltpu.roll(right[pl.ds(base, GROUP), :], LANES - 1, 1),
+    )
 
     for s in range(nspec, pad):
         state[pl.ds(s, GROUP, stride=pad), :] = jnp.zeros((GROUP, LANES), jnp.float32)
@@ -85,10 +90,9 @@
         after = jnp.where(at_bottom, bottom[s : s + 1, :], cells[s, pl.ds(row_below, 1), :])
         above = jnp.where(sub == 0, before, pltpu.roll(here, 1, 0))
         below = jnp.where(sub == GROUP - 1, after, pltpu.roll(here, GROUP - 1, 0))
-        edge_l = pltpu.roll(left_cols, LANES - 1 - s, 1)
-        edge_r = pltpu.roll(right_cols, (LANES - s) % LANES, 1) if s else right_cols
-        from_l = pltpu.roll(jnp.where(lane == LANES - 1, edge_l, here), 1, 1)
-        from_r = pltpu.roll(jnp.where(lane == 0, edge_r, here), LANES - 1, 1)
+        edge = pltpu.roll(edge_cols, LANES - 2 * s, 1) if s else edge_cols
+        from_l = jnp.where(lane == 0, edge, pltpu.roll(here, 1, 1))
+        from_r = jnp.where(lane == LANES - 1, edge, pltpu.roll(here, LANES - 1, 1))
         moved = here + coef[s] * ((above + below) + (from_l + from_r) - 4.0 * here)
         state[pl.ds(s, GROUP, stride=pad), :] = moved
 
@@ -123,18 +127,17 @@
                 mask = jnp.broadcast_to(step < counts[base + g], (pad, LANES))
                 pltpu.store(state.at[pl.ds(g * pad, pad), :], sums[:, k * LANES : (k + 1) * LANES], mask=mask)
 
-    def several(i, carry):
-        for u in range(UNROLL):
-            substep(i * UNROLL + u)
-        return carry
-
-    def single(i, carry):
-        substep(i)
-        return carry
-
-    whole = most // UNROLL
-    lax.fori_loop(0, whole, several, 0)
-    lax.fori_loop(whole * UNROLL, most, single, 0)
+    def run(count, start):
+        def steps(i, step):
+            for u in range(count):
+                substep(step + u)
+            return step + count
+
+        return lax.fori_loop(0, (most - start) // count, steps, start)
+
+    done = 0
+    for count in UNROLLS:
+        done = run(count, done)
 
     for s in range(nspec):
         out[s] = state[pl.ds(s, GROUP, stride=pad), :]
@@ -151,26 +154,23 @@
         pairs = [(i, (i + 1) % count) if up else ((i + 1) % count, i) for i in range(count)]
         return lax.ppermute(values, axis, pairs)
 
-    first_col, last_col, first_row, last_row = pl.pallas_call(
+    whole = pl.BlockSpec(memory_space=pltpu.VMEM)
+    near, cols, first_row, last_row = pl.pallas_call(
         functools.partial(edges_kernel, nspec),
         name="edges",
-        grid=(rows // EDGE_ROWS,),
-        in_specs=[pl.BlockSpec((nspec, EDGE_ROWS, lanes), lambda i: (0, i, 0))],
-        out_specs=[
-            pl.BlockSpec((EDGE_ROWS, lanes), lambda i: (i, 0)),
-            pl.BlockSpec((EDGE_ROWS, lanes), lambda i: (i, 0)),
-            pl.BlockSpec((nspec, lanes), lambda i: (0, 0)),
-            pl.BlockSpec((nspec, lanes), lambda i: (0, 0)),
-        ],
-        out_shape=[jax.ShapeDtypeStruct((rows, lanes), f32)] * 2 + [jax.ShapeDtypeStruct((nspec, lanes), f32)] * 2,
+        in_specs=[pl.BlockSpec(memory_space=pltpu.HBM)],
+        out_specs=[whole] * 4,
+        out_shape=[jax.ShapeDtypeStruct((nspec, rows, lanes), f32), jax.ShapeDtypeStruct((rows, lanes), f32)]
+        + [jax.ShapeDtypeStruct((nspec, lanes), f32)] * 2,
+        scratch_shapes=[pltpu.SemaphoreType.DMA((CHUNKS,))],
         compiler_params=pltpu.CompilerParams(vmem_limit_bytes=8 << 20),
         cost_estimate=pl.CostEstimate(flops=1 << 20, bytes_accessed=4 << 20, transcendentals=0),
-    )(cells)
-
+    )(pltpu.with_memory_space_constraint(cells, pltpu.HBM))
+
+    left = shift(cols, "pencil", True)
+    right = shift(cols, "pencil", False)
     top = shift(last_row, "space", True)
     bottom = shift(first_row, "space", False)
-    left = shift(last_col, "pencil", True)
-    right = shift(first_col, "pencil", False)
 
     lhs = pl.pallas_call(
         functools.partial(matrices_kernel, nspec, pad),
@@ -206,7 +206,7 @@
         ),
         compiler_params=pltpu.CompilerParams(vmem_limit_bytes=24 << 20),
         cost_estimate=pl.CostEstimate(flops=20 * rows * 2 * pad * 256 * 256, bytes_accessed=9 << 20, transcendentals=0),
-    )(substeps.reshape(rows), diffusivity, cells, top, bottom, left, right, lhs, reaction_rate)
+    )(substeps.reshape(rows), diffusivity, near, top, bottom, left, right, lhs, reaction_rate)
     return result.transpose(1, 0, 2)
 
 

time: 74.2 us -> 56.1 us (0.76)
  the two profiles are of different devices: /device:TPU:96 before, /device:TPU:1 now
where the time goes in v2:
time: 56.1 us; the launch traced here: 55.7 us
  Pallas kernels  46.8 us (83%)
  starting transfers between devices  8.83 us (16%)
    pallas_call x1, Pallas kernels, body(): pl.pallas_call(functools.partial(react_kernel, nspec, pad), name='react',...  41.5 us
    ppermute x4, starting transfers between devices, shift(): return lax.ppermute(values, axis, pairs)  8.83 us
    pallas_call x1, Pallas kernels, body(): pl.pallas_call(functools.partial(matrices_kernel, nspec, pad), name='matr...  2.74 us
    pallas_call x1, Pallas kernels, body(): pl.pallas_call(functools.partial(edges_kernel, nspec), name='edges', in_s...  2.52 us
  transfers between devices with their start and end apart: 4, of which 0 were waited for; matrix products, arithmetic and copies ran while one was open for 0% of the time, Pallas kernels for 5%

profile of v2, /device:TPU:1, one launch (start us, length us, event | category | flops | bytes accessed | tf_op | source)
XLA Modules:
  0.0 55.7 jit_solution(3339298065780695759)
XLA Ops:
  0.0 0.0 copy-start
  0.0 0.0 copy-start.1
  0.0 0.0 copy-start.2
  0.0 0.0 copy-start.3
  0.0 2.5 %edges.1 = (f32[53,128,128]{2,1,0:T(8,128)S(1)}, f32[128,128]{1,0:T(8,128)S(1)}, f32[53,128]{1,0:T(8,128)S(1)}, f32[53,128]{1,0:T(8,128)S(1)}) custom-call(f32[53,128,128]{2,1,0:T(8,128)} %bitcast.4), custom_call_target="tpu_custom_call" | custom-call | flops 1048576 | bytes 4194304 | tf_op jit(solution)/shard_map/edges/pallas_call | solution.py:158
  2.5 1.4 %collective-permute-start.3 = (f32[128,128]{1,0:T(8,128)S(1)}, f32[128,128]{1,0:T(8,128)S(1)}, u32[]{:S(2)}, u32[]{:S(2)}) collective-permute-start(f32[128,128]{1,0:T(8,128)S(1)} %get-tuple-element.12), channel_id=1, source_target_pairs={{1,0},{2,1},{3,2},{4,3},{5,4},{6,5},{7,6},{0,7},{9,8},{10,9},{11,1... | collective-permute-start | bytes 196616 | tf_op jit(solution)/shard_map/ppermute | solution.py:155
  3.9 1.2 %collective-permute-start.2 = (f32[128,128]{1,0:T(8,128)S(1)}, f32[128,128]{1,0:T(8,128)S(1)}, u32[]{:S(2)}, u32[]{:S(2)}) collective-permute-start(f32[128,128]{1,0:T(8,128)S(1)} %get-tuple-element.12), channel_id=1, source_target_pairs={{0,1},{1,2},{2,3},{3,4},{4,5},{5,6},{6,7},{7,0},{8,9},{9,10},{10,1... | collective-permute-start | bytes 196616 | tf_op jit(solution)/shard_map/ppermute | solution.py:155
  5.2 1.3 %collective-permute-start = (f32[53,128]{1,0:T(8,128)S(1)}, f32[53,128]{1,0:T(8,128)S(1)}, u32[]{:S(2)}, u32[]{:S(2)}) collective-permute-start(f32[53,128]{1,0:T(8,128)S(1)} %get-tuple-element.10), channel_id=1, source_target_pairs={{0,8},{8,16},{16,24},{24,32},{32,40},{40,48},{48,56},{56,64},{64,7... | collective-permute-start | bytes 81416 | tf_op jit(solution)/shard_map/ppermute | solution.py:155
  6.5 4.9 %collective-permute-start.1 = (f32[53,128]{1,0:T(8,128)S(1)}, f32[53,128]{1,0:T(8,128)S(1)}, u32[]{:S(2)}, u32[]{:S(2)}) collective-permute-start(f32[53,128]{1,0:T(8,128)S(1)} %get-tuple-element.11), channel_id=1, source_target_pairs={{8,0},{16,8},{24,16},{32,24},{40,32},{48,40},{56,48},{64,56},{72,6... | collective-permute-start | bytes 81416 | tf_op jit(solution)/shard_map/ppermute | solution.py:155
  11.4 0.0 copy-done
  11.4 2.7 %matrices.1.lhs = bf16[64,112,256]{2,1,0:T(8,128)(2,1)S(1)} custom-call(f32[128,2809]{1,0:T(8,128)S(1)} %copy-done), custom_call_target="tpu_custom_call" | custom-call | flops 16777216 | bytes 6291456 | tf_op jit(solution)/shard_map/matrices/pallas_call | solution.py:175
  14.1 0.0 collective-permute-done.top
  14.1 0.0 collective-permute-done.1.bottom
  14.2 0.0 collective-permute-done.3.right
  14.2 0.0 collective-permute-done.2.left
  14.2 0.0 copy-done.1
  14.2 0.0 copy-done.2
  14.2 0.0 copy-done.3
  14.2 41.5 %react.1 = f32[53,128,128]{2,1,0:T(8,128)} custom-call(s32[128]{0:T(128)S(1)} %bitcast.3, f32[53]{0:T(128)S(1)} %copy-done.3, f32[53,128,128]{2,1,0:T(8,128)S(1)} %get-tuple-element.9.cells, f32[53,128]{1,0:T(8,128)S(1)} %collective-permute-done.top, f32[53,128]{1,0:T(8,128)S(1)} %collective-permute-done.1.bottom, ...), custom_call_target="tpu_custom_call" | custom-call | flops 18790481920 | bytes 9437184 | tf_op jit(solution)/shard_map/react/pallas_call | solution.py:188
Async XLA Ops:
  0.0 11.4 %copy-start = (f32[128,2809]{1,0:T(8,128)S(1)}, f32[128,2809]{1,0:T(8,128)}, u32[]{:S(2)}) copy-start(f32[128,2809]{1,0:T(8,128)} %prop.1) | copy-start | bytes 4314628
  0.0 14.2 %copy-start.1 = (f32[128,128]{1,0:T(8,128)S(1)}, f32[128,128]{1,0:T(8,128)}, u32[]{:S(2)}) copy-start(f32[128,128]{1,0:T(8,128)} %rate.1) | copy-start | bytes 196612
  0.0 14.2 %copy-start.2 = (s32[128,1]{0,1:T(1,128)S(1)}, s32[128,1]{0,1:T(1,128)}, u32[]{:S(2)}) copy-start(s32[128,1]{0,1:T(1,128)} %param.9) | copy-start | bytes 1540
  0.0 14.2 %copy-start.3 = (f32[53]{0:T(128)S(1)}, f32[53]{0:T(128)}, u32[]{:S(2)}) copy-start(f32[53]{0:T(128)} %coef.1) | copy-start | bytes 640
  2.5 11.6 %collective-permute-start.3 = (f32[128,128]{1,0:T(8,128)S(1)}, f32[128,128]{1,0:T(8,128)S(1)}, u32[]{:S(2)}, u32[]{:S(2)}) collective-permute-start(f32[128,128]{1,0:T(8,128)S(1)} %get-tuple-element.12), channel_id=1, source_target_pairs={{1,0},{2,1},{3,2},{4,3},{5,4},{6,5},{7,6},{0,7},{9,8},{10,9},{11,1... | collective-permute-start | bytes 196616 | tf_op jit(solution)/shard_map/ppermute | solution.py:155
  3.9 10.2 %collective-permute-start.2 = (f32[128,128]{1,0:T(8,128)S(1)}, f32[128,128]{1,0:T(8,128)S(1)}, u32[]{:S(2)}, u32[]{:S(2)}) collective-permute-start(f32[128,128]{1,0:T(8,128)S(1)} %get-tuple-element.12), channel_id=1, source_target_pairs={{0,1},{1,2},{2,3},{3,4},{4,5},{5,6},{6,7},{7,0},{8,9},{9,10},{10,1... | collective-permute-start | bytes 196616 | tf_op jit(solution)/shard_map/ppermute | solution.py:155
  5.2 9.0 %collective-permute-start = (f32[53,128]{1,0:T(8,128)S(1)}, f32[53,128]{1,0:T(8,128)S(1)}, u32[]{:S(2)}, u32[]{:S(2)}) collective-permute-start(f32[53,128]{1,0:T(8,128)S(1)} %get-tuple-element.10), channel_id=1, source_target_pairs={{0,8},{8,16},{16,24},{24,32},{32,40},{40,48},{48,56},{56,64},{64,7... | collective-permute-start | bytes 81416 | tf_op jit(solution)/shard_map/ppermute | solution.py:155
  6.5 7.7 %collective-permute-start.1 = (f32[53,128]{1,0:T(8,128)S(1)}, f32[53,128]{1,0:T(8,128)S(1)}, u32[]{:S(2)}, u32[]{:S(2)}) collective-permute-start(f32[53,128]{1,0:T(8,128)S(1)} %get-tuple-element.11), channel_id=1, source_target_pairs={{8,0},{16,8},{24,16},{32,24},{40,32},{48,40},{56,48},{64,56},{72,6... | collective-permute-start | bytes 81416 | tf_op jit(solution)/shard_map/ppermute | solution.py:155
